TPU v7x, 32 devices: a whole 2x2x4 slice. The times are simulated.
32 devices in a mesh: dp: 2 (over x), ctx: 4 (over y, core), tp: 4 (over z).
Axes of the slice: x: 2, y: 2, z: 4, core: 2. Of those that a mesh axis runs over, the one named last changes fastest.
Arguments:
- tokens: bfloat16 [2, 4096, 768], P('dp', 'ctx'), may hold values from -6 to 6
- time_steps: int32 [2], P('dp'), may hold values from 0 to 999
- lengths: int32 [2], P('dp'), may hold values from 2048 to 4096, as said below
- time_table: bfloat16 [1000, 768], P(None, 'dp'), may hold values from -3 to 3
- norm_gains: bfloat16 [2, 768], P(None, 'dp'), may hold values from 0.5 to 1.5
- norm_biases: bfloat16 [2, 768], P(None, 'dp'), may hold values from -1 to 1
- w_qkv: bfloat16 [3, 768, 768], P(None, 'dp', 'tp'), may hold values from -0.3125 to 0.3125
- b_qv: bfloat16 [2, 768], P(None, 'tp'), may hold values from -0.099609375 to 0.099609375
- w_out: bfloat16 [768, 768], P('tp', 'dp'), may hold values from -0.3125 to 0.3125
- out_biases: bfloat16 [2, 768], P(None, 'dp'), may hold values from -1.25 to 1.25
- w_up: bfloat16 [768, 3072], P('dp', 'tp'), may hold values from -0.21875 to 0.21875
- b_up: bfloat16 [3072], P('tp'), may hold values from -1 to 1
- w_down: bfloat16 [3072, 768], P('tp', 'dp'), may hold values from -0.109375 to 0.109375
- cotangent: bfloat16 [2, 4096, 768], P('dp', 'ctx'), may hold values from -6 to 6
Outputs:
- layer_out: bfloat16 [2, 4096, 768], P('dp', 'ctx')
- grad_tokens: float32 [2, 4096, 768], P('dp', 'ctx')
- grad_time_table: float32 [1000, 768], P(None, 'dp')
- grad_norm_gains: float32 [2, 768], P(None, 'dp')
- grad_norm_biases: float32 [2, 768], P(None, 'dp')
- grad_w_qkv: float32 [3, 768, 768], P(None, 'dp', 'tp')
- grad_b_qv: float32 [2, 768], P(None, 'tp')
- grad_w_out: float32 [768, 768], P('tp', 'dp')
- grad_out_biases: float32 [2, 768], P(None, 'dp')
- grad_w_up: float32 [768, 3072], P('dp', 'tp')
- grad_b_up: float32 [3072], P('tp')
- grad_w_down: float32 [3072, 768], P('tp', 'dp')
Inputs may be any that keep to these rules, and one draw needn't show every extreme that they name: `lengths`: every sequence has 2048 to 4096 real tokens at its start, the rest padding; some sequence has exactly 4096.
All inputs are finite; a program needn't handle non-finite values.
Results may differ from a plain program's by a relative error of at most 0.019.
Values may be sent and summed in bfloat16 or wider, within the bound.
No kernel may reach another device: no remote copies, remote signals or barrier semaphores. Data moves between devices by JAX's collectives and lax.ppermute only.
A program may use at most 128 MiB of HBM per device.

v0:
```python
import math

import jax
import jax.numpy as jnp
from jax import lax
from jax.sharding import PartitionSpec as P

HEAD = 64


norm_eps = 1e-05


def normalize(values, gain_row, shift_row):
    center = values - jnp.mean(values, axis=-1, keepdims=True)
    spread = jnp.mean(center * center, axis=-1, keepdims=True)
    return center * lax.rsqrt(spread + norm_eps) * gain_row + shift_row


def gelu_exact(values):
    return jax.nn.gelu(values, approximate=False)


def on_device(
    tokens,
    time_steps,
    lengths,
    time_table,
    norm_gains,
    norm_biases,
    w_qkv,
    b_qv,
    w_out,
    out_biases,
    w_up,
    b_up,
    w_down,
    cotangent,
):
    seq_count, row_count, model_width = tokens.shape
    total_rows = seq_count * row_count
    ctx_rank = lax.axis_index("ctx")
    table_full, gains_full, shifts_full, qkv_full, proj_full, biases_full, up_full, down_full = (
        lax.all_gather(time_table, "dp", axis=1, tiled=True),
        lax.all_gather(norm_gains, "dp", axis=1, tiled=True),
        lax.all_gather(norm_biases, "dp", axis=1, tiled=True),
        lax.all_gather(w_qkv, "dp", axis=1, tiled=True),
        lax.all_gather(w_out, "dp", axis=1, tiled=True),
        lax.all_gather(out_biases, "dp", axis=1, tiled=True),
        lax.all_gather(w_up, "dp", axis=0, tiled=True),
        lax.all_gather(w_down, "dp", axis=1, tiled=True),
    )
    local_width = qkv_full.shape[2]
    head_local = local_width // HEAD
    score_scale = HEAD ** (-0.5)
    gains_wide = gains_full.astype(jnp.float32)
    shifts_wide = shifts_full.astype(jnp.float32)
    biases_wide = biases_full.astype(jnp.float32)
    qv_bias = b_qv.astype(jnp.float32)
    up_bias = b_up.astype(jnp.float32)
    steps_onehot = (time_steps[:, None] == jnp.arange(time_table.shape[0])[None, :]).astype(
        jnp.bfloat16
    )
    embedded = jnp.dot(steps_onehot, table_full, preferred_element_type=jnp.float32)
    start_rows = (tokens.astype(jnp.float32) + embedded[:, None, :]).reshape(
        total_rows, model_width
    )
    normed = normalize(start_rows, gains_wide[0], shifts_wide[0]).astype(jnp.bfloat16)
    projected = jnp.einsum("rd,idc->irc", normed, qkv_full, preferred_element_type=jnp.float32)
    query_rows = (projected[0] + qv_bias[0]).astype(jnp.bfloat16)
    key_rows = projected[1].astype(jnp.bfloat16)
    value_rows = (projected[2] + qv_bias[1]).astype(jnp.bfloat16)
    queries = query_rows.reshape(seq_count, row_count, head_local, HEAD)
    keys_all, values_all = (
        lax.all_gather(
            key_rows.reshape(seq_count, row_count, local_width), "ctx", axis=1, tiled=True
        ),
        lax.all_gather(
            value_rows.reshape(seq_count, row_count, local_width), "ctx", axis=1, tiled=True
        ),
    )
    key_total = keys_all.shape[1]
    key_block = math.gcd(key_total, 512)
    block_count = key_total // key_block
    key_valid = jnp.arange(key_total)[None, :] < lengths[:, None]

    def block_scores(block_index):
        offset = block_index * key_block
        key_piece = lax.dynamic_slice_in_dim(keys_all, offset, key_block, 1).reshape(
            seq_count, key_block, head_local, HEAD
        )
        value_piece = lax.dynamic_slice_in_dim(values_all, offset, key_block, 1).reshape(
            seq_count, key_block, head_local, HEAD
        )
        mask_piece = lax.dynamic_slice_in_dim(key_valid, offset, key_block, 1)[:, None, None, :]
        scores = (
            jnp.einsum("sqhe,skhe->shqk", queries, key_piece, preferred_element_type=jnp.float32)
            * score_scale
        )
        return (jnp.where(mask_piece, scores, -1e30), mask_piece, key_piece, value_piece)

    def running_stats(block_index, state_pair):
        running_peak, running_total = state_pair
        scores, mask_piece, key_piece, value_piece = block_scores(block_index)
        new_peak = jnp.maximum(running_peak, jnp.max(scores, axis=-1))
        shifted = jnp.where(mask_piece, jnp.exp(scores - new_peak[..., None]), 0.0)
        return (
            new_peak,
            running_total * jnp.exp(running_peak - new_peak) + jnp.sum(shifted, axis=-1),
        )

    start_peak = jnp.full((seq_count, head_local, row_count), -1e30, jnp.float32)
    running_peak, running_total = lax.fori_loop(
        0, block_count, running_stats, (start_peak, jnp.zeros_like(start_peak))
    )
    log_total = running_peak + jnp.log(running_total)

    def weighted_values(block_index, summed):
        scores, mask_piece, key_piece, value_piece = block_scores(block_index)
        weights = jnp.where(mask_piece, jnp.exp(scores - log_total[..., None]), 0.0).astype(
            jnp.bfloat16
        )
        return summed + jnp.einsum(
            "shqk,skhe->sqhe", weights, value_piece, preferred_element_type=jnp.float32
        )

    attended = lax.fori_loop(
        0,
        block_count,
        weighted_values,
        jnp.zeros((seq_count, row_count, head_local, HEAD), jnp.float32),
    )
    attended_low = attended.reshape(total_rows, local_width).astype(jnp.bfloat16)
    attn_part = jnp.dot(attended_low, proj_full, preferred_element_type=jnp.float32)
    middle = (
        start_rows
        + lax.psum(attn_part.astype(jnp.bfloat16), "tp").astype(jnp.float32)
        + biases_wide[0]
    )
    second = normalize(middle, gains_wide[1], shifts_wide[1]).astype(jnp.bfloat16)
    hidden = jnp.dot(second, up_full, preferred_element_type=jnp.float32) + up_bias
    activated = gelu_exact(hidden).astype(jnp.bfloat16)
    mlp_part = jnp.dot(activated, down_full, preferred_element_type=jnp.float32)
    result = (
        middle + lax.psum(mlp_part.astype(jnp.bfloat16), "tp").astype(jnp.float32) + biases_wide[1]
    )
    layer_out = result.reshape(seq_count, row_count, model_width).astype(jnp.bfloat16)
    positions = ctx_rank * row_count + jnp.arange(row_count)
    valid_rows = (positions[None, :] < lengths[:, None]).astype(jnp.float32)
    upstream = (cotangent.astype(jnp.float32) * valid_rows[:, :, None]).reshape(
        total_rows, model_width
    )
    upstream_low = upstream.astype(jnp.bfloat16)
    grad_down = jnp.einsum("rf,rd->fd", activated, upstream_low, preferred_element_type=jnp.float32)
    grad_bias_down = jnp.sum(upstream_low.astype(jnp.float32), axis=0)
    activation_back = jnp.einsum(
        "rd,fd->rf", upstream_low, down_full, preferred_element_type=jnp.float32
    )
    hidden_back = jax.vjp(gelu_exact, hidden)[1](activation_back)[0].astype(jnp.bfloat16)
    grad_up = jnp.einsum("rd,rf->df", second, hidden_back, preferred_element_type=jnp.float32)
    grad_bias_up = jnp.sum(hidden_back.astype(jnp.float32), axis=0)
    second_back = lax.psum(
        jnp.einsum("rf,df->rd", hidden_back, up_full, preferred_element_type=jnp.float32).astype(
            jnp.bfloat16
        ),
        "tp",
    ).astype(jnp.float32)
    middle_norm, gain_second, shift_second = jax.vjp(
        normalize, middle, gains_wide[1], shifts_wide[1]
    )[1](second_back)
    middle_back = upstream + middle_norm
    middle_low = middle_back.astype(jnp.bfloat16)
    grad_proj = jnp.einsum(
        "rc,rd->cd", attended_low, middle_low, preferred_element_type=jnp.float32
    )
    grad_bias_attn = jnp.sum(middle_low.astype(jnp.float32), axis=0)
    output_back = jnp.einsum(
        "rd,cd->rc", middle_low, proj_full, preferred_element_type=jnp.float32
    ).astype(jnp.bfloat16)
    output_back = output_back.reshape(seq_count, row_count, head_local, HEAD)
    row_delta = jnp.swapaxes(jnp.sum(output_back.astype(jnp.float32) * attended, axis=-1), 1, 2)

    def gradient_block(block_index, state_triple):
        query_grad, key_grads, value_grads = state_triple
        scores, mask_piece, key_piece, value_piece = block_scores(block_index)
        weights = jnp.where(mask_piece, jnp.exp(scores - log_total[..., None]), 0.0)
        weight_grad = jnp.einsum(
            "sqhe,skhe->shqk", output_back, value_piece, preferred_element_type=jnp.float32
        )
        score_grad = (weights * (weight_grad - row_delta[..., None])).astype(jnp.bfloat16)
        query_grad = query_grad + jnp.einsum(
            "shqk,skhe->sqhe", score_grad, key_piece, preferred_element_type=jnp.float32
        )
        key_part = (
            jnp.einsum("shqk,sqhe->skhe", score_grad, queries, preferred_element_type=jnp.float32)
            * score_scale
        )
        value_part = jnp.einsum(
            "shqk,sqhe->skhe",
            weights.astype(jnp.bfloat16),
            output_back,
            preferred_element_type=jnp.float32,
        )
        offset = block_index * key_block
        key_grads = lax.dynamic_update_slice_in_dim(
            key_grads, key_part.reshape(seq_count, key_block, local_width), offset, 1
        )
        value_grads = lax.dynamic_update_slice_in_dim(
            value_grads, value_part.reshape(seq_count, key_block, local_width), offset, 1
        )
        return (query_grad, key_grads, value_grads)

    zero_keys = jnp.zeros((seq_count, key_total, local_width), jnp.float32)
    query_grad, key_grads, value_grads = lax.fori_loop(
        0, block_count, gradient_block, (jnp.zeros_like(attended), zero_keys, zero_keys)
    )
    key_mine, value_mine = (
        lax.psum_scatter(
            key_grads.astype(jnp.bfloat16), "ctx", scatter_dimension=1, tiled=True
        ).astype(jnp.float32),
        lax.psum_scatter(
            value_grads.astype(jnp.bfloat16), "ctx", scatter_dimension=1, tiled=True
        ).astype(jnp.float32),
    )
    query_low = (query_grad * score_scale).reshape(total_rows, local_width).astype(jnp.bfloat16)
    key_low = key_mine.reshape(total_rows, local_width).astype(jnp.bfloat16)
    value_low = value_mine.reshape(total_rows, local_width).astype(jnp.bfloat16)
    stacked = jnp.stack((query_low, key_low, value_low))
    grad_qkv = jnp.einsum("rd,irc->idc", normed, stacked, preferred_element_type=jnp.float32)
    grad_bias_qv = jnp.stack(
        (
            jnp.sum(query_low.astype(jnp.float32), axis=0),
            jnp.sum(value_low.astype(jnp.float32), axis=0),
        )
    )
    normed_back = lax.psum(
        jnp.einsum("irc,idc->rd", stacked, qkv_full, preferred_element_type=jnp.float32).astype(
            jnp.bfloat16
        ),
        "tp",
    ).astype(jnp.float32)
    start_norm, gain_first, shift_first = jax.vjp(
        normalize, start_rows, gains_wide[0], shifts_wide[0]
    )[1](normed_back)
    grad_tokens = (middle_back + start_norm).reshape(seq_count, row_count, model_width)
    sequence_sums = jnp.sum(grad_tokens, axis=1)
    grad_table = jnp.einsum(
        "st,sd->td",
        steps_onehot.astype(jnp.float32),
        sequence_sums,
        precision=lax.Precision.HIGHEST,
    )
    gradients = (
        grad_table,
        jnp.stack((gain_first, gain_second)),
        jnp.stack((shift_first, shift_second)),
        grad_qkv,
        grad_proj,
        jnp.stack((grad_bias_attn, grad_bias_down)),
        grad_up,
        grad_down,
    )
    shards = (
        lax.psum_scatter(
            gradients[0].astype(jnp.bfloat16), "dp", scatter_dimension=1, tiled=True
        ).astype(jnp.float32),
        lax.psum_scatter(
            gradients[1].astype(jnp.bfloat16), "dp", scatter_dimension=1, tiled=True
        ).astype(jnp.float32),
        lax.psum_scatter(
            gradients[2].astype(jnp.bfloat16), "dp", scatter_dimension=1, tiled=True
        ).astype(jnp.float32),
        lax.psum_scatter(
            gradients[3].astype(jnp.bfloat16), "dp", scatter_dimension=1, tiled=True
        ).astype(jnp.float32),
        lax.psum_scatter(
            gradients[4].astype(jnp.bfloat16), "dp", scatter_dimension=1, tiled=True
        ).astype(jnp.float32),
        lax.psum_scatter(
            gradients[5].astype(jnp.bfloat16), "dp", scatter_dimension=1, tiled=True
        ).astype(jnp.float32),
        lax.psum_scatter(
            gradients[6].astype(jnp.bfloat16), "dp", scatter_dimension=0, tiled=True
        ).astype(jnp.float32),
        lax.psum_scatter(
            gradients[7].astype(jnp.bfloat16), "dp", scatter_dimension=1, tiled=True
        ).astype(jnp.float32),
    )
    shards = (
        lax.psum(shards[0].astype(jnp.bfloat16), "ctx").astype(jnp.float32),
        lax.psum(shards[1].astype(jnp.bfloat16), "ctx").astype(jnp.float32),
        lax.psum(shards[2].astype(jnp.bfloat16), "ctx").astype(jnp.float32),
        lax.psum(shards[3].astype(jnp.bfloat16), "ctx").astype(jnp.float32),
        lax.psum(shards[4].astype(jnp.bfloat16), "ctx").astype(jnp.float32),
        lax.psum(shards[5].astype(jnp.bfloat16), "ctx").astype(jnp.float32),
        lax.psum(shards[6].astype(jnp.bfloat16), "ctx").astype(jnp.float32),
        lax.psum(shards[7].astype(jnp.bfloat16), "ctx").astype(jnp.float32),
    )
    bias_qv_total, bias_up_total = lax.psum((grad_bias_qv, grad_bias_up), ("dp", "ctx"))
    return (
        layer_out,
        grad_tokens,
        shards[0],
        shards[1],
        shards[2],
        shards[3],
        bias_qv_total,
        shards[4],
        shards[5],
        shards[6],
        bias_up_total,
        shards[7],
    )


def solution(mesh):
    in_specs = (
        P("dp", "ctx", None),
        P("dp"),
        P("dp"),
        P(None, "dp"),
        P(None, "dp"),
        P(None, "dp"),
        P(None, "dp", "tp"),
        P(None, "tp"),
        P("tp", "dp"),
        P(None, "dp"),
        P("dp", "tp"),
        P("tp"),
        P("tp", "dp"),
        P("dp", "ctx", None),
    )
    out_specs = (
        P("dp", "ctx", None),
        P("dp", "ctx", None),
        P(None, "dp"),
        P(None, "dp"),
        P(None, "dp"),
        P(None, "dp", "tp"),
        P(None, "tp"),
        P("tp", "dp"),
        P(None, "dp"),
        P("dp", "tp"),
        P("tp"),
        P("tp", "dp"),
    )
    return jax.shard_map(
        on_device, mesh=mesh, in_specs=in_specs, out_specs=out_specs, check_vma=False
    )
```

profile of v0, /device:TPU:0, one launch (start us, length us, event | category | flops | bytes accessed | tf_op | source)
XLA Modules:
  0.0 848.8 jit_solution(17473282413200012350)
XLA Ops:
  8.6 5.5 all_gather.31
  14.1 4.5 all_gather.32
  19.3 21.5 %all_gather.33 = bf16[3,768,192]{1,2,0:T(8,128)(2,1)S(1)} all-gather(bf16[3,384,192]{1,2,0:T(8,128)(2,1)} %param.26), channel_id=1, replica_groups=mesh['dp'=2,'ctx'=4,'tp'=4] {'dp'}, dimensions={1}, use_global_device_ids=true | all-gather | bytes 1327104 | tf_op jit(solution)/shard_map/all_gather | solution.py:47
  40.8 5.9 all-gather.6.cloned.1.call-done
  54.0 6.6 all_gather.36
  60.7 2.4 fusion.73
  63.3 11.1 %all-gather.10.cloned.1.call-done = bf16[1,4096,192]{1,2,0:T(8,128)(2,1)} async-done(((bf16[1,1024,192]{1,2,0:T(8,128)(2,1)}), bf16[1,4096,192]{1,2,0:T(8,128)(2,1)}) %all-gather.10.cloned.1.call-update) | async-done | bytes 1572880 | tf_op jit(solution)/shard_map/all_gather | solution.py:75
  74.5 34.1 %while.48 = (s32[]{:T(128)}, f32[1,3,1024]{2,1,0:T(4,128)S(1)}, f32[1,3,1024]{2,1,0:T(4,128)S(1)}, pred[1,4096]{1,0:T(4,128)(4,1)S(1)}, bf16[1,4096,192]{1,2,0:T...) while((s32[]{:T(128)}, f32[1,3,1024]{2,1,0:T(4,128)S(1)}, ...), condition=%wide.region_5.6_spmd.clone, body=%wide.region_2.5_spmd.clone.sunk | while | flops 213924864 | bytes 13727918 | solution.py:113
  108.6 27.0 %while.49 = (s32[]{:T(128)}, f32[1,1024,3,64]{1,3,2,0:T(8,128)S(1)}, bf16[1,4096,192]{1,2,0:T(8,128)(2,1)}, pred[1,4096]{1,0:T(4,128)(4,1)S(1)}, bf16[1,4096,192...) while((s32[]{:T(128)}, ...), condition=%wide.region_7.8_spmd.clone, body=%wide.region_6.7_spmd.clone.sunk | while | flops 410910720 | bytes 3159733 | solution.py:127
  109.7 2.3 fusion.126
  113.1 2.3 fusion.126
  116.5 2.3 fusion.126
  119.9 2.3 fusion.126
  123.2 2.3 fusion.126
  126.6 2.3 fusion.126
  130.0 2.3 fusion.126
  133.4 2.3 fusion.126
  139.5 4.5 all_gather.37
  145.9 61.6 %all-reduce.9.cloned.1.call-done = bf16[1024,768]{1,0:T(8,128)(2,1)} async-done(((bf16[1024,768]{1,0:T(8,128)(2,1)}), bf16[1024,768]{1,0:T(8,128)(2,1)}) %all-reduce.9.cloned.1.call-update) | async-done | bytes 1572880 | tf_op jit(solution)/shard_map/psum | solution.py:137
  207.4 2.2 fusion.64
  211.8 2.1 add_convert_fusion.2
  214.0 16.8 %all-gather.12.cloned.1.call-done = bf16[768,768]{1,0:T(8,128)(2,1)} async-done(((bf16[384,768]{1,0:T(8,128)(2,1)}), bf16[768,768]{1,0:T(8,128)(2,1)}) %all-gather.12.cloned.1.call-update) | async-done | bytes 1179664 | tf_op jit(solution)/shard_map/all_gather | solution.py:50
  230.8 11.1 %multiply_convert_fusion.1 = (bf16[1024,768]{1,0:T(8,128)(2,1)}, f32[1024,768]{1,0:T(8,128)}, f32[1024,768]{1,0:T(8,128)}) fusion(f32[768]{0:T(1024)} %convert_element_type.258, bf16[1024,768]{1,0:T(8,128)(2,1)} %add_convert_fusion.2, bf16[768,768]{1,0:T(8,128)(2,1)} %all-gather.12.cloned.1.call-done), kind=kOutput, calls=%fused_computation.74 | convolution fusion | flops 1259864064 | bytes 10619904 | tf_op jit(solution)/shard_map/dot_general | solution.py:141
  241.9 13.1 %all-gather.14.cloned.1.call-done = bf16[768,768]{1,0:T(8,128)(2,1)} async-done(((bf16[768,384]{1,0:T(8,128)(2,1)}), bf16[768,768]{1,0:T(8,128)(2,1)}) %all-gather.14.cloned.1.call-update) | async-done | bytes 1179664 | tf_op jit(solution)/shard_map/all_gather | solution.py:51
  255.0 6.7 convert_reduce_fusion
  262.8 2.6 convolution_convert_fusion
  265.6 68.8 %all-reduce.11.cloned.1.call-done = bf16[1024,768]{1,0:T(8,128)(2,1)} async-done(((bf16[1024,768]{1,0:T(8,128)(2,1)}), bf16[1024,768]{1,0:T(8,128)(2,1)}) %all-reduce.11.cloned.1.call-update) | async-done | bytes 1572880 | tf_op jit(solution)/shard_map/psum | solution.py:162
  334.5 4.1 fusion.35
  346.3 86.8 %while.50 = (s32[]{:T(128)}, f32[1,1024,3,64]{1,3,2,0:T(8,128)}, bf16[1,4096,192]{1,2,0:T(8,128)(2,1)}, bf16[1,4096,192]{1,2,0:T(8,128)(2,1)}, bf16[1,4096,192]{...) while((s32[]{:T(128)}, f32[1,1024,3,64]{1,3,2,0:T(8,128)}, ...), condition=%wide.region_17.18_spmd.clone, body=%wide.region_16.17_spmd.clone.sunk | while | flops 1026097152 | bytes 42015080 | solution.py:214
  351.7 2.5 multiply_convert_fusion.6
  362.5 2.5 multiply_convert_fusion.6
  373.4 2.5 multiply_convert_fusion.6
  384.2 2.5 multiply_convert_fusion.6
  395.1 2.5 multiply_convert_fusion.6
  405.9 2.5 multiply_convert_fusion.6
  416.8 2.5 multiply_convert_fusion.6
  427.6 2.5 multiply_convert_fusion.6
  433.9 4.4 convolution_convert_fusion.1
  439.0 21.4 %reduce-scatter.27.cloned.1.call-done = bf16[1,1024,192]{1,2,0:T(8,128)(2,1)} async-done(((bf16[1,4096,192]{1,2,0:T(8,128)(2,1)}), bf16[1,1024,192]{1,2,0:T(8,128)(2,1)}) %reduce-scatter.27.cloned.1.call-update) | async-done | bytes 393232 | tf_op jit(solution)/shard_map/reduce_scatter | solution.py:221
  460.4 30.6 %reduce-scatter.25.cloned.1.call-done = bf16[1,1024,192]{1,2,0:T(8,128)(2,1)} async-done(((bf16[1,4096,192]{1,2,0:T(8,128)(2,1)}), bf16[1,1024,192]{1,2,0:T(8,128)(2,1)}) %reduce-scatter.25.cloned.1.call-update) | async-done | bytes 393232 | tf_op jit(solution)/shard_map/reduce_scatter | solution.py:218
  491.1 4.0 bitcast_convert_fusion
  496.0 2.6 convolution_convert_fusion.6
  500.9 4.5 convolution_convert_fusion.3
  505.3 2.4 copy.41
  508.4 3.5 fusion.54
  511.9 3.4 copy.35
  515.4 4.1 reshape.419
  519.5 96.7 %all-reduce.13.cloned.1.call-done = (bf16[1024,768]{1,0:T(8,128)(2,1)}, bf16[1024,768]{1,0:T(8,128)(2,1)}) async-done(((bf16[1024,768]{1,0:T(8,128)(2,1)}, bf16[1024,768]{1,0:T(8,128)(2,1)}), (bf16[1024,768]{1,0:T(8,128)(2,1)}, bf16[1024,768]{1,0:T(8,128)(2,1)})) %all-reduce.13.cloned.1.call-update) | async-done | bytes 3145744 | tf_op jit(solution)/shard_map/psum | solution.py:145
  616.3 2.6 fusion.33
  618.9 2.7 fusion.36
  621.6 5.5 fusion.70
  629.1 4.5 convolution_convert_fusion.4
  639.2 16.1 %reduce-scatter.43.cloned.1.call-done = bf16[384,768]{1,0:T(8,128)(2,1)} async-done(((bf16[768,768]{1,0:T(8,128)(2,1)}), bf16[384,768]{1,0:T(8,128)(2,1)}) %reduce-scatter.43.cloned.1.call-update) | async-done | bytes 589840
  655.3 2.1 copy.42
  657.4 20.4 %reduce-scatter.37.cloned.1.call-done = bf16[384,576]{1,0:T(8,128)(2,1)} async-done(((bf16[768,576]{1,0:T(8,128)(2,1)}), bf16[384,576]{1,0:T(8,128)(2,1)}) %reduce-scatter.37.cloned.1.call-update) | async-done | bytes 442384
  681.1 25.0 %reduce-scatter.31.cloned.1.call-done = bf16[384,1000]{1,0:T(8,128)(2,1)} async-done(((bf16[768,1000]{1,0:T(8,128)(2,1)}), bf16[384,1000]{1,0:T(8,128)(2,1)}) %reduce-scatter.31.cloned.1.call-update) | async-done | bytes 768016
  706.1 2.3 copy.30
  708.4 22.2 %reduce-scatter.29.cloned.1.call-done = bf16[384,768]{1,0:T(8,128)(2,1)} async-done(((bf16[768,768]{1,0:T(8,128)(2,1)}), bf16[384,768]{1,0:T(8,128)(2,1)}) %reduce-scatter.29.cloned.1.call-update) | async-done | bytes 589840 | tf_op jit(solution)/shard_map/reduce_scatter | solution.py:282
  730.8 13.0 %reduce-scatter.41.cloned.1.call-done = bf16[384,2]{1,0:T(8,128)(2,1)} async-done(((bf16[768,2]{1,0:T(8,128)(2,1)}), bf16[384,2]{1,0:T(8,128)(2,1)}) %reduce-scatter.41.cloned.1.call-update) | async-done | bytes 1552
  745.0 13.5 %all-reduce = (f32[2,192]{1,0:T(2,128)}, f32[768]{0:T(1024)}) all-reduce(f32[2,192]{1,0:T(2,128)S(1)} %pad_maximum_fusion.6, f32[768]{0:T(1024)S(1)} %copy-done.60), channel_id=1, replica_groups=mesh['dp'=2,'ctx'=4,'tp'=4] {'dp','ctx'}, use_global_device_ids=true, to_apply=%region_38.39 | all-reduce | flops 1152 | bytes 9216 | tf_op jit(solution)/shard_map/psum | solution.py:299
  759.5 11.3 %reduce-scatter.35.cloned.1.call-done = bf16[384,2]{1,0:T(8,128)(2,1)} async-done(((bf16[768,2]{1,0:T(8,128)(2,1)}), bf16[384,2]{1,0:T(8,128)(2,1)}) %reduce-scatter.35.cloned.1.call-update) | async-done | bytes 1552
  771.8 6.5 all-reduce.2
  780.0 53.5 %all-reduce.15.cloned.1.call-done = (bf16[1000,384]{1,0:T(8,128)(2,1)}, bf16[3,384,192]{1,2,0:T(8,128)(2,1)}, bf16[192,384]{1,0:T(8,128)(2,1)}, bf16[384,768]{1,0:T(8,128)(2,1)}, bf16[768,384]{1,0:T(8,128)(2,1)}) async-done(((bf16[1000,384]{1,0:T(8,128)(2,1)}, bf16[3,384,192]{1,2,0:T(8,128)(2,1)}, bf16[192,384]{1,0:T(8,128)(2,1)}, bf16[384,768]{1,0:T(8,128)(2,1)}, bf16[768,384]{1,0:T(8,128)(2,1)}), ...) | async-done | bytes 2537488 | tf_op jit(solution)/shard_map/psum | solution.py:290
  835.3 2.4 convert_element_type.280
  (455 shorter events, 159.9 us)
Async XLA Ops:
  7.2 41.3 %copy-start = (bf16[1,1024,768]{2,1,0:T(8,128)(2,1)S(1)}, bf16[1,1024,768]{2,1,0:T(8,128)(2,1)}, u32[]{:S(2)}) copy-start(bf16[1,1024,768]{2,1,0:T(8,128)(2,1)} %param.20) | copy-start | bytes 4718596
  7.2 39.6 %all-gather.6.cloned.1.call-start = ((), (), s32[]{:S(2)}) async-start(), calls=%async_computation.10 | async-start | bytes 2304000 | tf_op jit(solution)/shard_map/all_gather | solution.py:44
  7.9 66.5 %all-gather.10.cloned.1.call-start = ((), (), s32[]{:S(2)}) async-start(), calls=%async_computation.12 | async-start | bytes 1966080 | tf_op jit(solution)/shard_map/all_gather | solution.py:75
  18.7 32.2 %copy-start.34 = (f32[768]{0:T(1024)}, f32[768]{0:T(1024)S(1)}, u32[]{:S(2)}) copy-start(f32[768]{0:T(1024)S(1)} %get-tuple-element.539) | copy-start | bytes 9220
  19.3 31.6 %copy-start.58 = (f32[768]{0:T(1024)}, f32[768]{0:T(1024)S(1)}, u32[]{:S(2)}) copy-start(f32[768]{0:T(1024)S(1)} %get-tuple-element.541) | copy-start | bytes 9220
  40.8 10.1 %copy-start.21 = (bf16[3,768,192]{1,2,0:T(8,128)(2,1)}, bf16[3,768,192]{1,2,0:T(8,128)(2,1)S(1)}, u32[]{:S(2)}) copy-start(bf16[3,768,192]{1,2,0:T(8,128)(2,1)S(1)} %all_gather.33) | copy-start | bytes 2654212
  48.9 2.1 copy-start.30
  49.6 3.7 copy-start.59
  53.2 55.4 %all-gather.8.cloned.1.call-start = ((), (), s32[]{:S(2)}) async-start(), calls=%async_computation.11 | async-start | bytes 1966080 | tf_op jit(solution)/shard_map/all_gather | solution.py:78
  60.7 75.1 %copy-start.19 = (bf16[192,768]{1,0:T(8,128)(2,1)}, bf16[192,768]{1,0:T(8,128)(2,1)S(1)}, u32[]{:S(2)}) copy-start(bf16[192,768]{1,0:T(8,128)(2,1)S(1)} %all_gather.36) | copy-start | bytes 884740
  63.3 144.2 %all-reduce.9.cloned.1.call-start = ((), (), s32[]{:S(2)}) async-start(), calls=%async_computation.13 | async-start | bytes 3145728 | tf_op jit(solution)/shard_map/psum | solution.py:137
  135.6 3.9 copy-start.50
  135.7 10.2 %copy-start.16 = (f32[1,1024,3,64]{1,3,2,0:T(8,128)}, f32[1,1024,3,64]{1,3,2,0:T(8,128)S(1)}, u32[]{:S(2)}) copy-start(f32[1,1024,3,64]{1,3,2,0:T(8,128)S(1)} %get-tuple-element.434) | copy-start | bytes 2359300
  135.7 10.2 %copy-start.29 = (pred[1,4096]{1,0:T(4,128)(4,1)}, pred[1,4096]{1,0:T(4,128)(4,1)S(1)}, u32[]{:S(2)}) copy-start(pred[1,4096]{1,0:T(4,128)(4,1)S(1)} %get-tuple-element.993) | copy-start | bytes 12292
  135.7 3.9 copy-start.62
  135.7 9.0 %copy-start.61 = (bf16[768]{0:T(1024)(128)(2,1)S(1)}, bf16[768]{0:T(1024)(128)(2,1)}, u32[]{:S(2)}) copy-start(bf16[768]{0:T(1024)(128)(2,1)} %param.31) | copy-start | bytes 4612
  138.3 92.5 %all-gather.12.cloned.1.call-start = ((), (), s32[]{:S(2)}) async-start(), calls=%async_computation.14 | async-start | bytes 1769472 | tf_op jit(solution)/shard_map/all_gather | solution.py:50
  138.9 116.1 %all-gather.14.cloned.1.call-start = ((), (), s32[]{:S(2)}) async-start(), calls=%async_computation.15 | async-start | bytes 1769472 | tf_op jit(solution)/shard_map/all_gather | solution.py:51
  139.5 195.0 %all-reduce.11.cloned.1.call-start = ((), (), s32[]{:S(2)}) async-start(), calls=%async_computation.16 | async-start | bytes 3145728 | tf_op jit(solution)/shard_map/psum | solution.py:162
  207.4 2.2 copy-start.1
  207.4 4.4 copy-start.48
  255.0 7.8 copy-start.63
  265.4 195.1 %reduce-scatter.27.cloned.1.call-start = ((), (), s32[]{:S(2)}) async-start(), calls=%async_computation.18 | async-start | bytes 1966080 | tf_op jit(solution)/shard_map/reduce_scatter | solution.py:221
  334.5 4.1 copy-start.39
  334.5 4.1 copy-start.9
  334.5 4.1 copy-start.33
  340.6 2.3 copy-start.17
  342.2 4.1 copy-start.11
  342.8 3.4 copy-start.26
  433.1 57.9 %reduce-scatter.25.cloned.1.call-start = ((), (), s32[]{:S(2)}) async-start(), calls=%async_computation.17 | async-start | bytes 1966080 | tf_op jit(solution)/shard_map/reduce_scatter | solution.py:218
  433.9 182.4 %all-reduce.13.cloned.1.call-start = ((), (), s32[]{:S(2)}) async-start(), calls=%async_computation.27 | async-start | bytes 6291456 | tf_op jit(solution)/shard_map/psum | solution.py:145
  433.9 4.4 copy-start.4
  439.0 52.0 %copy-start.28 = (bf16[1,1024,3,64]{1,3,2,0:T(8,128)(2,1)}, bf16[1,1024,3,64]{1,3,2,0:T(8,128)(2,1)S(1)}, u32[]{:S(2)}) copy-start(bf16[1,1024,3,64]{1,3,2,0:T(8,128)(2,1)S(1)} %get-tuple-element.604) | copy-start | bytes 1179652
  495.0 5.8 copy-start.43
  495.1 142.4 %reduce-scatter.39.cloned.1.call-start = ((), (), s32[]{:S(2)}) async-start(), calls=%async_computation.24 | async-start | bytes 589824
  500.5 154.8 %reduce-scatter.43.cloned.1.call-start = ((), (), s32[]{:S(2)}) async-start(), calls=%async_computation.26 | async-start | bytes 1769472
  505.3 3.1 copy-start.24
  505.3 3.1 copy-start.31
  505.3 3.1 copy-start.35
  507.8 170.1 %reduce-scatter.37.cloned.1.call-start = ((), (), s32[]{:S(2)}) async-start(), calls=%async_computation.23 | async-start | bytes 1474560
  515.4 103.5 %copy-start.37 = (f32[1024]{0:T(1024)S(1)}, f32[1024]{0:T(1024)}, u32[]{:S(2)}) copy-start(f32[1024]{0:T(1024)} %copy-done.36) | copy-start | bytes 12292
  515.4 103.5 %copy-start.41 = (f32[1024]{0:T(1024)S(1)}, f32[1024]{0:T(1024)}, u32[]{:S(2)}) copy-start(f32[1024]{0:T(1024)} %copy-done.40) | copy-start | bytes 12292
  519.5 186.7 %reduce-scatter.31.cloned.1.call-start = ((), (), s32[]{:S(2)}) async-start(), calls=%async_computation.20 | async-start | bytes 2359296
  616.3 2.6 copy-start.7
  616.3 5.3 copy-start.6
  616.3 5.3 copy-start.13
  616.3 5.3 copy-start.44
  616.3 5.3 copy-start.46
  616.3 5.3 copy-start.52
  621.6 5.5 copy-start.49
  629.0 4.6 copy-start.10
  629.0 4.9 copy-start.53
  629.1 4.9 copy-start.55
  629.1 5.0 copy-start.54
  629.1 101.6 %reduce-scatter.29.cloned.1.call-start = ((), (), s32[]{:S(2)}) async-start(), calls=%async_computation.19 | async-start | bytes 1769472 | tf_op jit(solution)/shard_map/reduce_scatter | solution.py:282
  633.6 110.2 %reduce-scatter.41.cloned.1.call-start = ((), (), s32[]{:S(2)}) async-start(), calls=%async_computation.25 | async-start | bytes 294912
  634.9 123.6 %reduce-scatter.33.cloned.1.call-start = ((), (), s32[]{:S(2)}) async-start(), calls=%async_computation.21 | async-start | bytes 294912
  636.2 134.6 %reduce-scatter.35.cloned.1.call-start = ((), (), s32[]{:S(2)}) async-start(), calls=%async_computation.22 | async-start | bytes 294912
  637.1 196.4 %all-reduce.15.cloned.1.call-start = ((), (), s32[]{:S(2)}) async-start(), calls=%async_computation.28 | async-start | bytes 5074944 | tf_op jit(solution)/shard_map/psum | solution.py:290
  657.4 73.3 %copy-start.56 = (f32[3,64]{1,0:T(4,128)S(1)}, f32[3,64]{1,0:T(4,128)}, u32[]{:S(2)}) copy-start(f32[3,64]{1,0:T(4,128)} %get-tuple-element.603) | copy-start | bytes 2308
  657.4 87.4 %copy-start.25 = (bf16[1,1024,192]{1,2,0:T(8,128)(2,1)S(1)}, bf16[1,1024,192]{1,2,0:T(8,128)(2,1)}, u32[]{:S(2)}) copy-start(bf16[1,1024,192]{1,2,0:T(8,128)(2,1)} %reduce-scatter.27.cloned.1.call-done) | copy-start | bytes 1179652
  679.7 65.3 %copy-start.60 = (f32[768]{0:T(1024)S(1)}, f32[768]{0:T(1024)}, u32[]{:S(2)}) copy-start(f32[768]{0:T(1024)} %get-tuple-element.624) | copy-start | bytes 9220
  833.5 6.1 copy-start.23
  833.5 7.2 copy-start.22
  (55 other events, 67.7 us)
Sparse Core Ops, SparseCore 0:
  9.5 37.1 all-gather.5
  53.3 21.1 all-gather.9
  76.6 19.6 all-gather.7
  138.4 68.9 all-reduce.8
  208.8 21.9 all-gather.11
  232.2 22.7 all-gather.13
  265.5 68.9 all-reduce.10
  433.2 27.1 reduce-scatter.26
  463.0 28.0 reduce-scatter.24
  495.2 121.0 all-reduce.12
  618.5 12.1 reduce-scatter.38
  633.4 21.8 reduce-scatter.42
  658.1 19.6 reduce-scatter.36
  680.0 26.1 reduce-scatter.30
  708.8 21.8 reduce-scatter.28
  732.8 11.0 reduce-scatter.40
  746.5 11.1 reduce-scatter.32
  759.7 11.0 reduce-scatter.34
  774.7 58.7 all-reduce.14
where the time goes:
time: 857 us; the launch traced here: 849 us
  waiting for transfers between devices  491 us (57%)
  matrix products  134 us (16%)
  local copies, waits for them, and re-layouts  84.7 us (10%)
  blocking collectives  62.6 us (7%)
  other arithmetic  57.6 us (7%)
  between operations  16.6 us (2%)
    psum x1, waiting for transfers between devices, on_device(): lax.psum(mlp_part.astype(jnp.bfloat16), 'tp').astype(jnp.float32)  96.7 us
    unnamed x26, waiting for transfers between devices  88.6 us
    psum x1, waiting for transfers between devices, on_device(): lax.psum(jnp.einsum('rf,df->rd', hidden_back, up_full, preferred_element_...  68.8 us
    psum x1, waiting for transfers between devices, on_device(): lax.psum(attn_part.astype(jnp.bfloat16), 'tp').astype(jnp.float32)  61.6 us
    psum x1, waiting for transfers between devices, on_device(): lax.psum(shards[0].astype(jnp.bfloat16), 'ctx').astype(jnp.float32)  53.5 us
    unnamed x136, local copies, waits for them, and re-layouts  34.1 us
    reduce_scatter x1, waiting for transfers between devices, on_device(): lax.psum_scatter(key_grads.astype(jnp.bfloat16), 'ctx', scatter_dimension...  30.6 us
    dynamic_slice x24, local copies, waits for them, and re-layouts, block_scores(): lax.dynamic_slice_in_dim(keys_all, offset, key_block, 1)  23.6 us
  transfers between devices with their start and end apart: 19, of which 16 were waited for; matrix products, arithmetic and copies ran while one was open for 14% of the time, Pallas kernels for 0%

commit v1 on v0

v1 whole, which is shorter than its diff:
```python
import functools

import jax
import jax.numpy as jnp
from jax import lax
from jax.experimental import pallas as pl
from jax.experimental.pallas import tpu as pltpu
from jax.sharding import PartitionSpec as P

HEAD = 64
norm_eps = 1e-05
NT = (((1,), (1,)), ((), ()))
NN = (((1,), (0,)), ((), ()))
f32 = jnp.float32
bf16 = jnp.bfloat16
KERNEL_VMEM = 60 * 2**20


def dot(a, b, dims=NN):
    return lax.dot_general(a, b, dims, preferred_element_type=f32)


def attend_body(heads, piece, blocks, first, last, q_ref, *refs):
    kv_refs, bias_refs, refs = refs[:blocks], refs[blocks : 2 * blocks], refs[2 * blocks :]
    if first:
        out_ref, stat_ref, score_ref = refs
    else:
        part_ref, old_ref, out_ref, stat_ref, score_ref = refs
    rows = q_ref.shape[0]
    length = kv_refs[0].shape[1]
    width = heads * HEAD
    pieces = [(b, c) for b in range(blocks) for c in range(0, length, piece)]
    stats = []
    for h in range(heads):
        cols = slice(h * HEAD, (h + 1) * HEAD)
        vals = slice(width + h * HEAD, width + (h + 1) * HEAD)
        q = q_ref[:, cols]
        peak = None
        for b, c in pieces:
            scores = dot(q, kv_refs[b][cols, c : c + piece]) + bias_refs[b][:, c : c + piece]
            score_ref[h, :, b * length + c : b * length + c + piece] = scores
            for j in range(0, piece, 128):
                part = scores[:, j : j + 128]
                peak = part if peak is None else jnp.maximum(peak, part)
        peak = jnp.max(peak, axis=1, keepdims=True)
        if not first:
            old_peak = old_ref[:, h : h + 1]
            peak = jnp.maximum(peak, old_peak)
        total, summed = None, None
        for b, c in pieces:
            weights = jnp.exp(score_ref[h, :, b * length + c : b * length + c + piece] - peak)
            for j in range(0, piece, 128):
                part = weights[:, j : j + 128]
                total = part if total is None else total + part
            part = dot(weights.astype(bf16), kv_refs[b][vals, c : c + piece], NT)
            summed = part if summed is None else summed + part
        total = jnp.sum(total, axis=1, keepdims=True)
        if not first:
            shrink = jnp.exp(old_peak - peak)
            total = total + old_ref[:, 8 + h : 9 + h] * shrink
            summed = summed + part_ref[:, cols] * shrink
        if last:
            summed = summed / total
        stats.append((peak, total))
        out_ref[:, cols] = summed
    lane = lax.broadcasted_iota(jnp.int32, (rows, 128), 1)
    packed = jnp.zeros((rows, 128), f32)
    for h, (peak, total) in enumerate(stats):
        if last:
            packed = jnp.where(lane == h, peak + jnp.log(total), packed)
        else:
            packed = jnp.where(lane == h, peak, packed)
            packed = jnp.where(lane == 8 + h, total, packed)
    stat_ref[...] = packed


def row_spec(rows, width):
    return pl.BlockSpec((rows, width), lambda i: (i, 0))


def whole_spec(array):
    zeros = (0,) * array.ndim
    return pl.BlockSpec(array.shape, lambda i: zeros)


def attend(queries, kvs, biases, carry, last, rows=256, piece=512):
    count, width = queries.shape
    length = kvs[0].shape[1]
    heads = width // HEAD
    keys = length * len(kvs)
    args = [queries, *kvs, *biases]
    specs = [row_spec(rows, width)] + [whole_spec(a) for a in args[1:]]
    if carry is not None:
        args += list(carry)
        specs += [row_spec(rows, width), row_spec(rows, 128)]
    return pl.pallas_call(
        functools.partial(attend_body, heads, piece, len(kvs), carry is None, last),
        grid=(count // rows,),
        in_specs=specs,
        out_specs=[row_spec(rows, width), row_spec(rows, 128)],
        out_shape=[
            jax.ShapeDtypeStruct((count, width), f32),
            jax.ShapeDtypeStruct((count, 128), f32),
        ],
        scratch_shapes=[pltpu.VMEM((heads, rows, keys), f32)],
        cost_estimate=pl.CostEstimate(
            flops=16 * count * keys * width,
            bytes_accessed=count * width * 6 + keys * width * 4,
            transcendentals=count * keys * heads,
        ),
        compiler_params=pltpu.CompilerParams(vmem_limit_bytes=KERNEL_VMEM),
        name="attend",
    )(*args)


def attend_back_body(heads, piece, blocks, first, q_ref, do_ref, att_ref, log_ref, *refs):
    kv_refs, bias_refs, refs = refs[:blocks], refs[blocks : 2 * blocks], refs[2 * blocks :]
    if not first:
        part_ref, refs = refs[0], refs[1:]
    dq_ref, dkv_refs, sum_refs = refs[0], refs[1 : 1 + blocks], refs[1 + blocks :]
    step = pl.program_id(0)
    length = kv_refs[0].shape[1]
    width = heads * HEAD

    @pl.when(step == 0)
    def _():
        for sum_ref in sum_refs:
            sum_ref[...] = jnp.zeros_like(sum_ref)

    q, do = q_ref[...], do_ref[...]
    q_t, do_t = q.T, do.T
    product = do.astype(f32) * att_ref[...]
    for h in range(heads):
        cols = slice(h * HEAD, (h + 1) * HEAD)
        vals = slice(width + h * HEAD, width + (h + 1) * HEAD)
        delta = jnp.sum(product[:, cols], axis=1, keepdims=True)
        log_total = log_ref[:, h : h + 1]
        dq = None
        for b in range(blocks):
            for c in range(0, length, piece):
                span = slice(c, c + piece)
                scores = dot(q[:, cols], kv_refs[b][cols, span]) + bias_refs[b][:, span]
                probs = jnp.exp(scores - log_total)
                grads = dot(do[:, cols], kv_refs[b][vals, span])
                score_grad = (probs * (grads - delta)).astype(bf16)
                part = dot(score_grad, kv_refs[b][cols, span], NT)
                dq = part if dq is None else dq + part
                sum_refs[b][cols, span] += dot(q_t[cols, :], score_grad)
                sum_refs[b][vals, span] += dot(do_t[cols, :], probs.astype(bf16))
        dq = dq * HEAD ** (-0.5)
        if not first:
            dq = dq + part_ref[:, cols]
        dq_ref[:, cols] = dq.astype(dq_ref.dtype)

    @pl.when(step == pl.num_programs(0) - 1)
    def _():
        for dkv_ref, sum_ref in zip(dkv_refs, sum_refs):
            dkv_ref[...] = sum_ref[...].astype(dkv_ref.dtype)


def attend_back(queries, do, att, log_total, kvs, biases, part, rows=512, piece=1024):
    count, width = queries.shape
    length = kvs[0].shape[1]
    heads = width // HEAD
    keys = length * len(kvs)
    args = [queries, do, att, log_total, *kvs, *biases]
    specs = [row_spec(rows, width)] * 3 + [row_spec(rows, 128)]
    specs += [whole_spec(a) for a in args[4:]]
    if part is not None:
        args.append(part)
        specs.append(row_spec(rows, width))
    return pl.pallas_call(
        functools.partial(attend_back_body, heads, piece, len(kvs), part is None),
        grid=(count // rows,),
        in_specs=specs,
        out_specs=[row_spec(rows, width)] + [whole_spec(kv) for kv in kvs],
        out_shape=[jax.ShapeDtypeStruct((count, width), f32 if part is None else bf16)]
        + [jax.ShapeDtypeStruct(kv.shape, bf16) for kv in kvs],
        scratch_shapes=[pltpu.VMEM(kv.shape, f32) for kv in kvs],
        cost_estimate=pl.CostEstimate(
            flops=40 * count * keys * width,
            bytes_accessed=count * width * 12 + keys * width * 8,
            transcendentals=count * keys * heads,
        ),
        compiler_params=pltpu.CompilerParams(vmem_limit_bytes=KERNEL_VMEM),
        name="attend_back",
    )(*args)


def middle_body(
    num_ref, att_ref, tok_ref, emb_ref, par_ref, bup_ref, cot_ref, wout_ref, w_ref,
    layer_ref, back_ref, do_ref, grad_ref, vec_ref, bvec_ref,
    mid_ref, sec_ref, sect_ref, upl_ref, uplt_ref, mlp_ref, sback_ref,
):
    step = pl.program_id(0)
    tps, rows, width = att_ref.shape
    model = tok_ref.shape[1]
    wide = w_ref.shape[2] // 2

    @pl.when(step == 0)
    def _():
        start = tok_ref[...].astype(f32) + emb_ref[...]
        attn = None
        for t in range(tps):
            part = dot(att_ref[t], wout_ref[t][:, :width], NT)
            attn = part if attn is None else attn + part
        middle = start + attn + par_ref[2:3, :]
        mid_ref[...] = middle
        center = middle - jnp.mean(middle, axis=1, keepdims=True)
        scale = lax.rsqrt(jnp.mean(center * center, axis=1, keepdims=True) + norm_eps)
        second = (center * scale * par_ref[0:1, :] + par_ref[1:2, :]).astype(bf16)
        sec_ref[...] = second
        sect_ref[...] = second.T
        place = num_ref[0] + lax.broadcasted_iota(jnp.int32, (rows, model), 0)
        upstream = jnp.where(place < num_ref[1], cot_ref[...].astype(f32), 0.0)
        low = upstream.astype(bf16)
        upl_ref[...] = low
        uplt_ref[...] = low.T
        mlp_ref[...] = jnp.zeros_like(mlp_ref)
        sback_ref[...] = jnp.zeros_like(sback_ref)

    w_up, w_down = w_ref[0, :, :wide], w_ref[0, :, wide:]
    hidden = dot(sec_ref[...], w_up) + bup_ref[pl.ds(step, 1), :]
    half = 0.5 * (1.0 + lax.erf(hidden * (0.5**0.5)))
    activated = (hidden * half).astype(bf16)
    mlp_ref[...] += dot(activated, w_down, NT)
    act_back = dot(upl_ref[...], w_down)
    slope = half + hidden * (jnp.exp(-0.5 * hidden * hidden) * 0.3989422804014327)
    hidden_back = (act_back * slope).astype(bf16)
    sback_ref[...] += dot(hidden_back, w_up, NT)
    bvec_ref[pl.ds(step, 1), :] = jnp.sum(hidden_back.astype(f32), axis=0, keepdims=True)
    grad_ref[pl.ds(step, 1), :, :wide] = dot(sect_ref[...], hidden_back).astype(bf16)[None]
    grad_ref[pl.ds(step, 1), :, wide : 2 * wide] = dot(uplt_ref[...], activated).astype(bf16)[None]

    @pl.when(step == pl.num_programs(0) - 1)
    def _():
        middle = mid_ref[...]
        layer_ref[...] = (middle + mlp_ref[...] + par_ref[3:4, :]).astype(bf16)
        center = middle - jnp.mean(middle, axis=1, keepdims=True)
        scale = lax.rsqrt(jnp.mean(center * center, axis=1, keepdims=True) + norm_eps)
        n = center * scale
        e = sback_ref[...]
        eg = e * par_ref[0:1, :]
        norm = scale * (
            eg
            - jnp.mean(eg, axis=1, keepdims=True)
            - n * jnp.mean(eg * n, axis=1, keepdims=True)
        )
        upstream = upl_ref[...].astype(f32)
        back = upstream + norm
        back_ref[...] = back
        low = back.astype(bf16)
        low_t = low.T
        for t in range(tps):
            do_ref[t] = dot(low, wout_ref[t][:, :width]).astype(bf16)
            grad_ref[t, :, 2 * wide : 2 * wide + width] = dot(low_t, att_ref[t]).astype(bf16)
        vec_ref[0:1, :] = jnp.sum(e * n, axis=0, keepdims=True)
        vec_ref[1:2, :] = jnp.sum(e, axis=0, keepdims=True)
        vec_ref[2:3, :] = jnp.sum(low.astype(f32), axis=0, keepdims=True)
        vec_ref[3:4, :] = jnp.sum(upstream, axis=0, keepdims=True)
        vec_ref[4:8, :] = jnp.zeros((4, model), f32)


def middle_part(numbers, att, tokens, embedded, params, b_up, cotangent, weights):
    tps, rows, width = att.shape
    model = tokens.shape[1]
    packed = weights.shape[2]
    wide = b_up.shape[1]
    fixed = lambda shape: pl.BlockSpec(shape, lambda i, n: (0,) * len(shape))
    mine = pl.BlockSpec((rows, model), lambda i, n: (n[2], 0))
    spare = packed - 2 * wide
    return pl.pallas_call(
        middle_body,
        grid_spec=pltpu.PrefetchScalarGridSpec(
            num_scalar_prefetch=1,
            grid=(tps,),
            in_specs=[
                fixed(att.shape),
                mine,
                fixed(embedded.shape),
                fixed(params.shape),
                fixed(b_up.shape),
                mine,
                pl.BlockSpec((tps, model, spare), lambda i, n: (0, 0, 2 * wide // spare)),
                pl.BlockSpec((1, model, 2 * wide), lambda i, n: (i, 0, 0)),
            ],
            out_specs=[
                fixed((rows, model)),
                fixed((rows, model)),
                fixed(att.shape),
                fixed(weights.shape),
                fixed((8, model)),
                fixed(b_up.shape),
            ],
            scratch_shapes=[
                pltpu.VMEM((rows, model), f32),
                pltpu.VMEM((rows, model), bf16),
                pltpu.VMEM((model, rows), bf16),
                pltpu.VMEM((rows, model), bf16),
                pltpu.VMEM((model, rows), bf16),
                pltpu.VMEM((rows, model), f32),
                pltpu.VMEM((rows, model), f32),
            ],
        ),
        out_shape=[
            jax.ShapeDtypeStruct((rows, model), bf16),
            jax.ShapeDtypeStruct((rows, model), f32),
            jax.ShapeDtypeStruct(att.shape, bf16),
            jax.ShapeDtypeStruct(weights.shape, bf16),
            jax.ShapeDtypeStruct((8, model), f32),
            jax.ShapeDtypeStruct(b_up.shape, f32),
        ],
        cost_estimate=pl.CostEstimate(
            flops=12 * rows * model * wide * tps,
            bytes_accessed=2 * weights.size * 2,
            transcendentals=2 * rows * wide * tps,
        ),
        compiler_params=pltpu.CompilerParams(vmem_limit_bytes=KERNEL_VMEM),
        name="middle",
    )(numbers, att, tokens, embedded, params, b_up, cotangent, weights, weights)


def shift(value, axis, size, by):
    return lax.ppermute(value, axis, [(i, (i + by) % size) for i in range(size)])


def flip(value, axis, size, bit):
    return lax.ppermute(value, axis, [(i, i ^ bit) for i in range(size)])


def swap_rows(value, tps):
    return lax.all_to_all(value, "tp", 0, 0, tiled=True)


def on_device(
    dps, ctxs, tps,
    tokens, time_steps, lengths, time_table, norm_gains, norm_biases, w_qkv, b_qv, w_out,
    out_biases, w_up, b_up, w_down, cotangent,
):
    _, row_count, model = tokens.shape
    local = b_qv.shape[1]
    heads = local // HEAD
    wide = b_up.shape[0]
    part = w_up.shape[0]
    steps_in_table = time_table.shape[0]
    rows = row_count // tps
    dp, ctx, tp = lax.axis_index("dp"), lax.axis_index("ctx"), lax.axis_index("tp")

    all_steps = lax.all_gather(time_steps, "dp", tiled=True)
    small = jnp.concatenate((norm_gains, norm_biases, out_biases, time_table[all_steps]))
    small = lax.all_gather(small, "dp", axis=1, tiled=True).astype(f32)
    embedded = lax.dynamic_slice_in_dim(small, 6 + dp, 1, 0)
    gain_first, shift_first = small[0:1], small[2:3]
    params = jnp.stack(
        (small[1], small[3], small[4], small[5], small[1], small[1], small[1], small[1])
    )

    qkv_mine = jnp.concatenate((w_qkv[0], w_qkv[1], w_qkv[2]), axis=1)
    qkv_full = lax.all_gather(qkv_mine, "dp", axis=0, tiled=True)
    slab = part // ctxs
    spare = -(-local // 128) * 128
    piece = jnp.concatenate(
        (
            lax.dynamic_slice_in_dim(w_up, ctx * slab, slab, 0),
            lax.dynamic_slice_in_dim(w_down, ctx * slab, slab, 1).T,
            jnp.pad(
                lax.dynamic_slice_in_dim(w_out, ctx * slab, slab, 1).T,
                ((0, 0), (0, spare - local)),
            ),
        ),
        axis=1,
    )
    weights = lax.all_gather(piece, ("tp", "dp", "ctx"), axis=0, tiled=True)
    weights = weights.reshape(tps, model, 2 * wide + spare)

    flat = tokens.reshape(row_count, model)
    start = flat.astype(f32) + embedded
    center = start - jnp.mean(start, axis=1, keepdims=True)
    scale = lax.rsqrt(jnp.mean(center * center, axis=1, keepdims=True) + norm_eps)
    normed = (center * scale * gain_first + shift_first).astype(bf16)
    bias = b_qv.astype(f32)
    kv_bias = jnp.concatenate((jnp.zeros((local,), f32), bias[1]))[:, None]
    kv = lax.dot_general(
        qkv_full[:, local:], normed, (((0,), (1,)), ((), ())), preferred_element_type=f32
    )
    kv = (kv + kv_bias).astype(bf16)
    queries = (dot(normed, qkv_full[:, :local]) + bias[0]).astype(bf16) * bf16(HEAD**-0.5)

    place = jnp.arange(row_count)[None, :]

    def key_bias(owner):
        return jnp.where(owner * row_count + place < lengths[0], 0.0, -1e30).astype(f32)

    biases = [key_bias(ctx ^ b) for b in range(4)]
    kv_1 = flip(kv, "ctx", ctxs, 1)
    kv_2 = flip(kv, "ctx", ctxs, 2)
    kv_3 = flip(kv_2, "ctx", ctxs, 1)
    carry = attend(queries, (kv, kv_1), biases[:2], None, False)
    attended, log_total = attend(queries, (kv_2, kv_3), biases[2:], carry, True)

    swapped = swap_rows(attended.astype(bf16).reshape(tps, rows, local), tps)
    numbers = jnp.stack((ctx * row_count + tp * rows, lengths[0], tp)).astype(jnp.int32)
    layer_rows, middle_back, output_back, grad_packed, vectors, grad_b_up = middle_part(
        numbers,
        swapped,
        flat,
        embedded,
        params,
        lax.all_gather(b_up.astype(bf16), "tp").astype(f32),
        cotangent.reshape(row_count, model),
        weights,
    )
    layer_out = lax.all_gather(layer_rows, "tp", axis=0, tiled=True)
    output_back = swap_rows(output_back, tps).reshape(row_count, local)

    grad_packed = lax.psum_scatter(
        grad_packed.reshape(tps * model, -1), ("tp", "dp", "ctx"), scatter_dimension=0, tiled=True
    )
    grad_packed = lax.all_gather(grad_packed, "ctx", axis=0, tiled=True).astype(f32)
    grad_w_up = grad_packed[:, :wide]
    grad_w_down = grad_packed[:, wide : 2 * wide].T
    grad_w_out = grad_packed[:, 2 * wide : 2 * wide + local].T

    dq, dkv_2, dkv_3 = attend_back(
        queries, output_back, attended, log_total, (kv_2, kv_3), biases[2:], None
    )
    far = (dkv_2.astype(f32) + flip(dkv_3, "ctx", ctxs, 1).astype(f32)).astype(bf16)
    far = flip(far, "ctx", ctxs, 2)
    dq, dkv_0, dkv_1 = attend_back(
        queries, output_back, attended, log_total, (kv, kv_1), biases[:2], dq
    )
    near = flip(dkv_1, "ctx", ctxs, 1)
    dkv = (dkv_0.astype(f32) + near.astype(f32) + far.astype(f32)).astype(bf16)

    back = dot(dq, qkv_full[:, :local], NT) + lax.dot_general(
        dkv, qkv_full[:, local:], (((0,), (1,)), ((), ())), preferred_element_type=f32
    )
    back = swap_rows(back.astype(bf16).reshape(tps, rows, model), tps)
    grad_qkv = jnp.concatenate(
        (
            lax.dot_general(normed, dq, (((0,), (0,)), ((), ())), preferred_element_type=f32),
            lax.dot_general(normed, dkv, (((0,), (1,)), ((), ())), preferred_element_type=f32),
        ),
        axis=1,
    ).astype(bf16)
    grad_qkv = lax.psum_scatter(grad_qkv, ("dp", "ctx"), scatter_dimension=0, tiled=True)
    grad_qkv = lax.all_gather(grad_qkv, "ctx", axis=0, tiled=True).astype(f32)
    grad_w_qkv = jnp.stack([grad_qkv[:, i * local : (i + 1) * local] for i in range(3)])

    e = jnp.sum(back.astype(f32), axis=0)
    mine = lax.dynamic_slice_in_dim(flat, tp * rows, rows, 0).astype(f32) + embedded
    center = mine - jnp.mean(mine, axis=1, keepdims=True)
    scale = lax.rsqrt(jnp.mean(center * center, axis=1, keepdims=True) + norm_eps)
    n = center * scale
    eg = e * gain_first
    start_norm = scale * (
        eg - jnp.mean(eg, axis=1, keepdims=True) - n * jnp.mean(eg * n, axis=1, keepdims=True)
    )
    grad_rows = middle_back + start_norm
    low_rows = grad_rows.astype(bf16)
    grad_tokens = jnp.zeros((row_count, model), f32)
    for by in range(tps):
        moved = low_rows if by == 0 else shift(low_rows, "tp", tps, by)
        grad_tokens = lax.dynamic_update_slice_in_dim(
            grad_tokens, moved.astype(f32), ((tp - by) % tps) * rows, 0
        )

    token_sums = jnp.zeros((dps, model), f32)
    token_sums = lax.dynamic_update_slice_in_dim(
        token_sums, jnp.sum(grad_rows, axis=0, keepdims=True), dp, 0
    )
    qv_sums = jnp.concatenate(
        (jnp.sum(dq.astype(f32), axis=0), jnp.sum(dkv[local:].astype(f32), axis=1))
    )
    qv_slots = jnp.zeros((tps, 2 * local), f32)
    qv_slots = lax.dynamic_update_slice_in_dim(qv_slots, qv_sums[None], tp, 0)
    sums = jnp.concatenate(
        (
            vectors[:4],
            jnp.sum(e * n, axis=0, keepdims=True),
            jnp.sum(e, axis=0, keepdims=True),
            token_sums,
            grad_b_up.reshape(-1, model),
            qv_slots.reshape(-1, model),
        )
    )
    sums = lax.psum(sums, ("dp", "ctx", "tp"))
    own = lax.dynamic_slice_in_dim(sums, dp * part, part, 1)
    grad_gains = jnp.stack((own[4], own[0]))
    grad_shifts = jnp.stack((own[5], own[1]))
    grad_out_biases = jnp.stack((own[2], own[3]))
    at = 6 + dps
    b_rows = grad_b_up.size // model
    grad_b_up = lax.dynamic_slice_in_dim(
        sums[at : at + b_rows].reshape(-1), tp * wide, wide, 0
    )
    grad_b_qv = lax.dynamic_index_in_dim(
        sums[at + b_rows :].reshape(tps, 2, local), tp, 0, False
    )
    step_rows = jnp.arange(steps_in_table)[:, None]
    grad_table = jnp.zeros((steps_in_table, part), f32)
    for s in range(dps):
        grad_table = grad_table + jnp.where(step_rows == all_steps[s], own[6 + s][None], 0.0)
    return (
        layer_out[None],
        grad_tokens[None],
        grad_table,
        grad_gains,
        grad_shifts,
        grad_w_qkv,
        grad_b_qv,
        grad_w_out,
        grad_out_biases,
        grad_w_up,
        grad_b_up,
        grad_w_down,
    )


def solution(mesh):
    in_specs = (
        P("dp", "ctx", None),
        P("dp"),
        P("dp"),
        P(None, "dp"),
        P(None, "dp"),
        P(None, "dp"),
        P(None, "dp", "tp"),
        P(None, "tp"),
        P("tp", "dp"),
        P(None, "dp"),
        P("dp", "tp"),
        P("tp"),
        P("tp", "dp"),
        P("dp", "ctx", None),
    )
    out_specs = (
        P("dp", "ctx", None),
        P("dp", "ctx", None),
        P(None, "dp"),
        P(None, "dp"),
        P(None, "dp"),
        P(None, "dp", "tp"),
        P(None, "tp"),
        P("tp", "dp"),
        P(None, "dp"),
        P("dp", "tp"),
        P("tp"),
        P("tp", "dp"),
    )
    sizes = (mesh.shape["dp"], mesh.shape["ctx"], mesh.shape["tp"])
    return jax.shard_map(
        functools.partial(on_device, *sizes),
        mesh=mesh,
        in_specs=in_specs,
        out_specs=out_specs,
        check_vma=False,
    )
```

time: 857 us -> 496 us (0.58)
  waiting for transfers between devices: 491 us -> 207 us
  matrix products: 134 us -> 7.68 us
  Pallas kernels: 0 us -> 88.6 us
  local copies, waits for them, and re-layouts: 84.7 us -> 27.4 us
  blocking collectives: 62.6 us -> 99.3 us
  other arithmetic: 57.6 us -> 21.3 us
  starting transfers between devices: 1.53 us -> 20 us
    psum x4 -> x0, waiting for transfers between devices: 281 us -> none  [the longest x1 96.7 us: on_device(): lax.psum(mlp_part.astype(jnp.bfloat16), 'tp').astype(jnp.float32)]
    dot_general x68 -> x6, matrix products: 132 us -> 7.68 us  [the longest x2 4.54 us: dot(): return lax.dot_general(a, b, dims, preferred_element_type=f32)]
    pallas_call x0 -> x5, Pallas kernels: none -> 88.6 us  [the longest x2 39.1 us: attend_back(): pl.pallas_call(functools.partial(attend_back_body, heads, piece, len(kvs)...]
    unnamed x26 -> x5, waiting for transfers between devices: 88.6 us -> 1.26 us
    reduce_scatter x3 -> x2, waiting for transfers between devices: 74.3 us -> 159 us  [the longest x1 136 us: on_device(): lax.psum_scatter(grad_packed.reshape(tps * model, -1), ('tp', 'dp', 'ctx'...]
    all_gather x5 -> x3, waiting for transfers between devices: 47 us -> 0.02 us  [the longest x1 0.02 us: on_device(): layer_out = lax.all_gather(layer_rows, 'tp', axis=0, tiled=True)]
    ppermute x0 -> x9, waiting for transfers between devices: none -> 36 us  [the longest x6 36 us: flip(): return lax.ppermute(value, axis, [(i, i ^ bit) for i in range(size)])]
    reduce_sum x23 -> x9, other arithmetic: 40.4 us -> 5.69 us  [the longest x1 2.08 us: on_device(): jnp.sum(e, axis=0, keepdims=True)]
  transfers between devices with their start and end apart: 19 -> 17, of which waited for: 16 -> 6; matrix products, arithmetic and copies ran while one was open for 14% -> 8% of each run, Pallas kernels for 0% -> 14%
where the time goes in v1:
time: 496 us; the launch traced here: 487 us
  waiting for transfers between devices  207 us (42%)
  blocking collectives  99.3 us (20%)
  Pallas kernels  88.6 us (18%)
  local copies, waits for them, and re-layouts  27.4 us (6%)
  other arithmetic  21.3 us (4%)
  starting transfers between devices  20 us (4%)
  between operations  16.2 us (3%)
  matrix products  7.68 us (2%)
    reduce_scatter x1, waiting for transfers between devices, on_device(): lax.psum_scatter(grad_packed.reshape(tps * model, -1), ('tp', 'dp', 'ctx'...  136 us
    psum x1, blocking collectives, on_device(): sums = lax.psum(sums, ('dp', 'ctx', 'tp'))  51.8 us
    pallas_call x2, Pallas kernels, attend_back(): pl.pallas_call(functools.partial(attend_back_body, heads, piece, len(kvs)...  39.1 us
    ppermute x6, waiting for transfers between devices, flip(): return lax.ppermute(value, axis, [(i, i ^ bit) for i in range(size)])  36 us
    pallas_call x2, Pallas kernels, attend(): pl.pallas_call(functools.partial(attend_body, heads, piece, len(kvs), car...  30 us
    reduce_scatter x1, waiting for transfers between devices, on_device(): lax.psum_scatter(grad_qkv, ('dp', 'ctx'), scatter_dimension=0, tiled=True)  22.6 us
    pallas_call x1, Pallas kernels, middle_part(): pl.pallas_call(middle_body, grid_spec=pltpu.PrefetchScalarGridSpec(num_sc...  19.5 us
    all_gather x1, blocking collectives, on_device(): lax.all_gather(b_up.astype(bf16), 'tp').astype(f32)  17.7 us
  transfers between devices with their start and end apart: 17, of which 6 were waited for; matrix products, arithmetic and copies ran while one was open for 8% of the time, Pallas kernels for 14%

profile of v1, /device:TPU:0, one launch (start us, length us, event | category | flops | bytes accessed | tf_op | source)
XLA Modules:
  0.0 487.2 jit_solution(7743351298899975588)
XLA Ops:
  7.3 1.2 constant_dynamic-slice_fusion.3
  8.7 0.9 constant_dynamic-slice_fusion.4
  9.6 1.1 constant_dynamic-slice_fusion.2
  10.8 0.8 fusion.21
  12.8 0.8 dynamic-update-slice
  13.6 5.2 %all-reduce.2 = s32[2]{0:T(128)S(1)} all-reduce(s32[2]{0:T(128)S(1)} %dynamic-update-slice), channel_id=1, replica_groups=mesh['dp'=2,'ctx'=4,'tp'=4] {'dp'}, use_global_device_ids=true, to_apply=%add.2 | all-reduce | flops 2 | bytes 16
  19.5 4.4 all_gather.28
  25.0 12.7 %all_gather.29 = bf16[768,576]{0,1:T(8,128)(2,1)S(1)} all-gather(bf16[384,576]{0,1:T(8,128)(2,1)S(1)} %pad_maximum_fusion.2), channel_id=1, replica_groups=mesh['dp'=2,'ctx'=4,'tp'=4] {'dp'}, dimensions={0}, use_global_device_ids=true | all-gather | bytes 1327104 | tf_op jit(solution)/shard_map/all_gather | solution.py:359
  37.7 0.7 multiply_reduce_fusion
  38.4 0.7 add_convert_fusion.1
  39.1 0.8 add_convert_fusion.4.refs_0_
  40.3 1.5 collective-permute-start
  42.4 2.8 fusion.3.q_ref
  45.2 18.6 %collective-permute-done.refs_0_ = bf16[384,1024]{1,0:T(8,128)(2,1)} collective-permute-done((bf16[384,1024]{1,0:T(8,128)(2,1)S(1)}, bf16[384,1024]{1,0:T(8,128)(2,1)}, u32[]{:S(2)}, u32[]{:S(2)}) %collective-permute-start) | collective-permute-done | bytes 786464 | tf_op jit(solution)/shard_map/ppermute | solution.py:328
  65.0 0.9 copy-done.22
  65.9 13.9 %attend.2 = (f32[1024,192]{1,0:T(8,128)}, f32[1024,128]{1,0:T(8,128)}) custom-call(bf16[1024,192]{1,0:T(8,128)(2,1)} %fusion.3.q_ref, bf16[384,1024]{1,0:T(8,128)(2,1)} %copy-done.21, bf16[384,1024]{1,0:T(8,128)(2,1)} %copy-done.22, f32[1,1024]{1,0:T(1,128)} %get-tuple-element.102.refs_2_, f32[1,1024]{1,0:T(1,128)} %get-tuple-element.101.refs_3_), custom_call_target="tpu_custom_call" | custom-call | flops 6442450944 | bytes 2752512 | tf_op jit(solution)/shard_map/attend/pallas_call | solution.py:96
  79.9 0.9 copy-done.23
  80.7 16.0 %attend.3 = (f32[1024,192]{1,0:T(8,128)}, f32[1024,128]{1,0:T(8,128)}) custom-call(bf16[1024,192]{1,0:T(8,128)(2,1)} %fusion.3.q_ref, bf16[384,1024]{1,0:T(8,128)(2,1)} %collective-permute-done.refs_0_, bf16[384,1024]{1,0:T(8,128)(2,1)} %copy-done.23, f32[1,1024]{1,0:T(1,128)} %get-tuple-element.104.refs_2_, f32[1,1024]{1,0:T(1,128)} %get-tuple-element.103.refs_3_, ...), custom_call_target="tpu_custom_call" | custom-call | flops 6442450944 | bytes 2752512 | tf_op jit(solution)/shard_map/attend/pallas_call | solution.py:96
  96.8 1.3 convert_element_type.85
  98.1 1.0 copy.32
  99.0 3.8 all-to-all-start
  103.5 17.7 %all-gather.1 = bf16[4,1,768]{2,1,0:T(2,128)(2,1)S(1)} all-gather(bf16[1,1,768]{2,1,0:T(2,128)(2,1)S(1)} %reshape.205), channel_id=2, replica_groups=mesh['dp'=2,'ctx'=4,'tp'=4] {'tp'}, dimensions={0}, use_global_device_ids=true | all-gather | bytes 7680 | tf_op jit(solution)/shard_map/all_gather | solution.py:409
  121.3 0.7 pad_add_fusion.num_ref
  122.5 1.0 copy.36.att_ref
  123.5 19.5 %middle.1 = (bf16[256,768]{1,0:T(8,128)(2,1)}, f32[256,768]{1,0:T(8,128)}, bf16[4,256,192]{2,1,0:T(8,128)(2,1)}, bf16[4,768,1792]{2,1,0:T(8,128)(2,1)}, f32[8,768]{1,0:T(8,128)}, /*index=5*/f32[4,768]{1,0:T(4,128)}) custom-call(s32[3]{0:T(128)} %pad_add_fusion.num_ref, bf16[4,256,192]{2,1,0:T(8,128)(2,1)} %copy.36.att_ref, bf16[1024,768]{1,0:T(8,128)(2,1)} %bitcast.74, ...), custom_call_target="tpu_custom_call" | custom-call | flops 7247757312 | bytes 22020096 | tf_op jit(solution)/shard_map/middle/pallas_call | solution.py:272
  143.1 2.0 copy.37
  145.1 3.5 all-to-all-start.1
  148.6 0.7 all-gather.8.cloned.1.call-update
  149.3 8.6 %all-to-all-done.1 = bf16[4,256,192]{1,2,0:T(8,128)(2,1)S(1)} async-done(((bf16[4,256,192]{1,2,0:T(8,128)(2,1)}), bf16[4,256,192]{1,2,0:T(8,128)(2,1)S(1)}, u32[]{:S(2)}, u32[]{:S(2)}) %all-to-all-start.1) | async-done | bytes 393248 | tf_op jit(solution)/shard_map/all_to_all | solution.py:332
  158.0 1.0 copy.38
  159.0 19.4 %attend_back.2 = (f32[1024,192]{1,0:T(8,128)}, bf16[384,1024]{1,0:T(8,128)(2,1)}, bf16[384,1024]{1,0:T(8,128)(2,1)}) custom-call(bf16[1024,192]{1,0:T(8,128)(2,1)} %fusion.3.q_ref, bf16[1024,192]{1,0:T(8,128)(2,1)} %bitcast.79, f32[1024,192]{1,0:T(8,128)} %get-tuple-element.30.att_ref, f32[1024,128]{1,0:T(8,128)} %get-tuple-element.34.log_ref, ...), custom_call_target="tpu_custom_call" | custom-call | flops 16106127360 | bytes 5505024 | tf_op jit(solution)/shard_map/attend_back/pallas_call | solution.py:172
  178.4 19.7 %attend_back.3 = (bf16[1024,192]{1,0:T(8,128)(2,1)}, bf16[384,1024]{1,0:T(8,128)(2,1)}, bf16[384,1024]{1,0:T(8,128)(2,1)}) custom-call(bf16[1024,192]{1,0:T(8,128)(2,1)} %fusion.3.q_ref, bf16[1024,192]{1,0:T(8,128)(2,1)} %bitcast.80, f32[1024,192]{1,0:T(8,128)} %get-tuple-element.30.att_ref, f32[1024,128]{1,0:T(8,128)} %get-tuple-element.34.log_ref, ...), custom_call_target="tpu_custom_call" | custom-call | flops 16106127360 | bytes 5505024 | tf_op jit(solution)/shard_map/attend_back/pallas_call | solution.py:172
  199.1 1.6 collective-permute-start.5
  201.2 17.4 %collective-permute-done.5 = bf16[384,1024]{1,0:T(8,128)(2,1)S(1)} collective-permute-done((bf16[384,1024]{1,0:T(8,128)(2,1)S(1)}, bf16[384,1024]{1,0:T(8,128)(2,1)S(1)}, u32[]{:S(2)}, u32[]{:S(2)}) %collective-permute-start.5) | collective-permute-done | bytes 786464 | tf_op jit(solution)/shard_map/ppermute | solution.py:328
  219.0 0.8 convolution_convert_fusion
  219.9 1.3 copy.46
  222.5 1.0 fusion.18
  223.5 1.7 add_convert_fusion
  225.2 4.5 all-to-all-start.2
  230.5 1.3 iota_compare_fusion.1
  232.7 22.6 %reduce-scatter.7.cloned.1.call-done = bf16[96,576]{1,0:T(8,128)(2,1)} async-done(((bf16[768,576]{1,0:T(8,128)(2,1)}), bf16[96,576]{1,0:T(8,128)(2,1)}) %reduce-scatter.7.cloned.1.call-update) | async-done | bytes 110608 | tf_op jit(solution)/shard_map/reduce_scatter | solution.py:446
  255.3 7.4 %all_gather.34 = bf16[384,576]{1,0:T(8,128)(2,1)S(1)} all-gather(bf16[96,576]{1,0:T(8,128)(2,1)} %reduce-scatter.7.cloned.1.call-done), channel_id=1, replica_groups=mesh['dp'=2,'ctx'=4,'tp'=4] {'ctx'}, dimensions={0}, use_global_device_ids=true | all-gather | bytes 552960 | tf_op jit(solution)/shard_map/all_gather | solution.py:447
  263.0 1.3 copy.42
  264.3 2.1 all-to-all-done.2
  266.4 2.1 convert_reduce_fusion
  268.9 136.3 %reduce-scatter.9.cloned.1.call-done = bf16[96,1792]{1,0:T(8,128)(2,1)} async-done(((bf16[3072,1792]{1,0:T(8,128)(2,1)}), bf16[96,1792]{1,0:T(8,128)(2,1)}) %reduce-scatter.9.cloned.1.call-update) | async-done | bytes 344080 | tf_op jit(solution)/shard_map/reduce_scatter | solution.py:416
  405.2 1.5 fusion.25
  406.7 1.9 broadcast_in_dim.107
  408.6 1.0 convert_dynamic-update-slice_fusion.3
  409.5 1.1 collective-permute-start.6
  410.6 1.7 collective-permute-start.7
  412.3 1.5 collective-permute-start.8
  414.0 51.8 %psum.7 = f32[14,768]{1,0:T(8,128)S(1)} all-reduce(f32[14,768]{1,0:T(8,128)S(1)} %concatenate.27), channel_id=1, replica_groups=mesh['dp'=2,'ctx'=4,'tp'=4] {'dp','ctx','tp'}, use_global_device_ids=true, to_apply=%region_12.13 | all-reduce | flops 10752 | bytes 86016 | tf_op jit(solution)/shard_map/psum | solution.py:487
  465.9 1.5 select_add_fusion
  469.3 0.7 dynamic_slice.32
  470.6 0.9 convert_dynamic-update-slice_fusion.2
  471.5 0.9 convert_dynamic-update-slice_fusion.1
  472.4 0.9 convert_dynamic-update-slice_fusion
  473.4 1.5 convert_element_type.102
  475.0 1.4 copy.44
  476.4 0.9 copy.43
  477.3 1.1 slice.144
  478.4 0.7 copy-done.8
  479.1 1.1 copy.63
  (135 shorter events, 13.9 us)
Async XLA Ops:
  7.2 11.7 %copy-start = (bf16[1000,384]{1,0:T(8,128)(2,1)S(1)}, bf16[1000,384]{1,0:T(8,128)(2,1)}, u32[]{:S(2)}) copy-start(bf16[1000,384]{1,0:T(8,128)(2,1)} %param.17) | copy-start | bytes 2304004
  7.2 5.1 %copy-start.24 = (u32[32]{0:T(128)S(1)}, u32[32]{0:T(128)}, u32[]{:S(2)}) copy-start(u32[32]{0:T(128)} %constant.113) | copy-start | bytes 388
  7.2 12.2 %copy-start.20 = (bf16[2,384]{1,0:T(2,128)(2,1)S(1)}, bf16[2,384]{1,0:T(2,128)(2,1)}, u32[]{:S(2)}) copy-start(bf16[2,384]{1,0:T(2,128)(2,1)} %param.18) | copy-start | bytes 4612
  7.2 12.2 %copy-start.19 = (bf16[2,384]{1,0:T(2,128)(2,1)S(1)}, bf16[2,384]{1,0:T(2,128)(2,1)}, u32[]{:S(2)}) copy-start(bf16[2,384]{1,0:T(2,128)(2,1)} %param.19) | copy-start | bytes 4612
  7.2 12.2 %copy-start.18 = (bf16[2,384]{1,0:T(2,128)(2,1)S(1)}, bf16[2,384]{1,0:T(2,128)(2,1)}, u32[]{:S(2)}) copy-start(bf16[2,384]{1,0:T(2,128)(2,1)} %param.23) | copy-start | bytes 4612
  7.2 16.6 %copy-start.16 = (bf16[2,192]{1,0:T(2,128)(2,1)S(1)}, bf16[2,192]{1,0:T(2,128)(2,1)}, u32[]{:S(2)}) copy-start(bf16[2,192]{1,0:T(2,128)(2,1)} %param.21) | copy-start | bytes 2308
  7.2 16.7 %copy-start.13 = (bf16[3,384,192]{1,2,0:T(8,128)(2,1)S(1)}, bf16[3,384,192]{1,2,0:T(8,128)(2,1)}, u32[]{:S(2)}) copy-start(bf16[3,384,192]{1,2,0:T(8,128)(2,1)} %param.20) | copy-start | bytes 1327108
  7.3 116.3 %all-gather.6.cloned.1.call-start = ((), (), s32[]{:S(2)}) async-start(), calls=%async_computation.5 | async-start | bytes 11354112 | tf_op jit(solution)/shard_map/all_gather | solution.py:373
  9.6 15.0 %copy-start.2 = (bf16[1,1024,768]{2,1,0:T(8,128)(2,1)S(1)}, bf16[1,1024,768]{2,1,0:T(8,128)(2,1)}, u32[]{:S(2)}) copy-start(bf16[1,1024,768]{2,1,0:T(8,128)(2,1)} %param.14) | copy-start | bytes 4718596
  37.7 4.7 copy-start.5
  39.1 1.1 copy-start.9
  40.3 5.0 %copy-start.21 = (bf16[384,1024]{1,0:T(8,128)(2,1)}, bf16[384,1024]{1,0:T(8,128)(2,1)S(1)}, u32[]{:S(2)}) copy-start(bf16[384,1024]{1,0:T(8,128)(2,1)S(1)} %add_convert_fusion.4.refs_0_) | copy-start | bytes 2359300
  40.3 23.6 %collective-permute-start = (bf16[384,1024]{1,0:T(8,128)(2,1)S(1)}, bf16[384,1024]{1,0:T(8,128)(2,1)}, u32[]{:S(2)}, u32[]{:S(2)}) collective-permute-start(bf16[384,1024]{1,0:T(8,128)(2,1)S(1)} %add_convert_fusion.4.refs_0_), channel_id=1, source_target_pairs={{0,8},{4,12},{8,0},{12,4},{1,9},{5,13},{9,1},{13,5},{2,10},{6,14},... | collective-permute-start | bytes 2359304 | tf_op jit(solution)/shard_map/ppermute | solution.py:328
  41.7 23.3 %collective-permute-start.2 = (bf16[384,1024]{1,0:T(8,128)(2,1)S(1)}, bf16[384,1024]{1,0:T(8,128)(2,1)S(1)}, u32[]{:S(2)}, u32[]{:S(2)}) collective-permute-start(bf16[384,1024]{1,0:T(8,128)(2,1)S(1)} %add_convert_fusion.4.refs_0_), channel_id=1, source_target_pairs={{0,4},{4,0},{8,12},{12,8},{1,5},{5,1},{9,13},{13,9},{2,6},{6,2},{1... | collective-permute-start | bytes 2359304 | tf_op jit(solution)/shard_map/ppermute | solution.py:328
  63.8 16.0 %collective-permute-start.1 = (bf16[384,1024]{1,0:T(8,128)(2,1)}, bf16[384,1024]{1,0:T(8,128)(2,1)S(1)}, u32[]{:S(2)}, u32[]{:S(2)}) collective-permute-start(bf16[384,1024]{1,0:T(8,128)(2,1)} %collective-permute-done.refs_0_), channel_id=1, source_target_pairs={{0,4},{4,0},{8,12},{12,8},{1,5},{5,1},{9,13},{13,9},{2,6},{6,2},{1... | collective-permute-start | bytes 2359304 | tf_op jit(solution)/shard_map/ppermute | solution.py:328
  65.0 0.9 copy-start.22
  79.9 0.9 copy-start.23
  96.8 6.1 %copy-start.17 = (bf16[768]{0:T(1024)(128)(2,1)S(1)}, bf16[768]{0:T(1024)(128)(2,1)}, u32[]{:S(2)}) copy-start(bf16[768]{0:T(1024)(128)(2,1)} %param.25) | copy-start | bytes 4612
  99.0 23.5 %all-to-all-start = ((bf16[4,256,192]{1,2,0:T(8,128)(2,1)}), bf16[4,256,192]{1,2,0:T(8,128)(2,1)S(1)}, u32[]{:S(2)}, u32[]{:S(2)}) async-start(bf16[4,256,192]{1,2,0:T(8,128)(2,1)} %copy.32), calls=%async_computation | async-start | bytes 786432 | tf_op jit(solution)/shard_map/all_to_all | solution.py:332
  145.1 12.9 %all-to-all-start.1 = ((bf16[4,256,192]{1,2,0:T(8,128)(2,1)}), bf16[4,256,192]{1,2,0:T(8,128)(2,1)S(1)}, u32[]{:S(2)}, u32[]{:S(2)}) async-start(bf16[4,256,192]{1,2,0:T(8,128)(2,1)} %copy.37), calls=%async_computation.1 | async-start | bytes 786432 | tf_op jit(solution)/shard_map/all_to_all | solution.py:332
  148.5 84.1 %all-gather.8.cloned.1.call-start = ((), (), s32[]{:S(2)}) async-start(), calls=%async_computation.6 | async-start | bytes 1966080 | tf_op jit(solution)/shard_map/all_gather | solution.py:413
  149.3 106.0 %reduce-scatter.7.cloned.1.call-start = ((), (), s32[]{:S(2)}) async-start(), calls=%async_computation.8 | async-start | bytes 1105920 | tf_op jit(solution)/shard_map/reduce_scatter | solution.py:446
  178.3 20.4 %collective-permute-start.4 = (bf16[384,1024]{1,0:T(8,128)(2,1)}, bf16[384,1024]{1,0:T(8,128)(2,1)S(1)}, u32[]{:S(2)}, u32[]{:S(2)}) collective-permute-start(bf16[384,1024]{1,0:T(8,128)(2,1)} %get-tuple-element.40), channel_id=1, source_target_pairs={{0,4},{4,0},{8,12},{12,8},{1,5},{5,1},{9,13},{13,9},{2,6},{6,2},{1... | collective-permute-start | bytes 2359304 | tf_op jit(solution)/shard_map/ppermute | solution.py:328
  178.4 20.3 %copy-start.12 = (bf16[384,1024]{1,0:T(8,128)(2,1)S(1)}, bf16[384,1024]{1,0:T(8,128)(2,1)}, u32[]{:S(2)}) copy-start(bf16[384,1024]{1,0:T(8,128)(2,1)} %get-tuple-element.39) | copy-start | bytes 2359300
  198.1 2.5 copy-start.7
  198.1 2.5 copy-start.10
  198.2 3.0 collective-permute-start.3
  199.1 19.5 %collective-permute-start.5 = (bf16[384,1024]{1,0:T(8,128)(2,1)S(1)}, bf16[384,1024]{1,0:T(8,128)(2,1)S(1)}, u32[]{:S(2)}, u32[]{:S(2)}) collective-permute-start(bf16[384,1024]{1,0:T(8,128)(2,1)S(1)} %add_convert_fusion.3), channel_id=1, source_target_pairs={{0,8},{4,12},{8,0},{12,4},{1,9},{5,13},{9,1},{13,5},{2,10},{6,14},... | collective-permute-start | bytes 2359304 | tf_op jit(solution)/shard_map/ppermute | solution.py:328
  200.7 17.9 %copy-start.11 = (bf16[384,1024]{1,0:T(8,128)(2,1)S(1)}, bf16[384,1024]{1,0:T(8,128)(2,1)}, u32[]{:S(2)}) copy-start(bf16[384,1024]{1,0:T(8,128)(2,1)} %get-tuple-element.37) | copy-start | bytes 2359300
  221.2 183.9 %reduce-scatter.9.cloned.1.call-start = ((), (), s32[]{:S(2)}) async-start(), calls=%async_computation.9 | async-start | bytes 11354112 | tf_op jit(solution)/shard_map/reduce_scatter | solution.py:416
  221.3 1.2 copy-start.6
  225.2 6.5 %copy-start.3 = (bf16[1,1024,768]{2,1,0:T(8,128)(2,1)S(1)}, bf16[1,1024,768]{2,1,0:T(8,128)(2,1)}, u32[]{:S(2)}) copy-start(bf16[1,1024,768]{2,1,0:T(8,128)(2,1)} %param.14) | copy-start | bytes 4718596
  225.2 7.0 %copy-start.15 = (f32[8,768]{1,0:T(8,128)S(1)}, f32[8,768]{1,0:T(8,128)}, u32[]{:S(2)}) copy-start(f32[8,768]{1,0:T(8,128)} %get-tuple-element.41) | copy-start | bytes 73732
  225.2 41.1 %all-to-all-start.2 = ((bf16[4,256,768]{2,1,0:T(8,128)(2,1)}), bf16[4,256,768]{2,1,0:T(8,128)(2,1)}, u32[]{:S(2)}, u32[]{:S(2)}) async-start(bf16[4,256,768]{2,1,0:T(8,128)(2,1)} %bitcast.19), calls=%async_computation.2 | async-start | bytes 3145728 | tf_op jit(solution)/shard_map/all_to_all | solution.py:332
  229.7 243.6 %all-gather.10.cloned.1.call-start = ((), (), s32[]{:S(2)}) async-start(), calls=%async_computation.7 | async-start | bytes 1720320 | tf_op jit(solution)/shard_map/all_gather | solution.py:419
  408.6 5.3 %copy-start.14 = (f32[4,768]{1,0:T(4,128)S(1)}, f32[4,768]{1,0:T(4,128)}, u32[]{:S(2)}) copy-start(f32[4,768]{1,0:T(4,128)} %get-tuple-element.42) | copy-start | bytes 36868
  409.5 61.1 %collective-permute-start.6 = (bf16[256,768]{1,0:T(8,128)(2,1)S(1)}, bf16[256,768]{1,0:T(8,128)(2,1)S(1)}, u32[]{:S(2)}, u32[]{:S(2)}) collective-permute-start(bf16[256,768]{1,0:T(8,128)(2,1)S(1)} %get-tuple-element.80), channel_id=1, source_target_pairs={{0,1},{1,2},{2,3},{3,0},{4,5},{5,6},{6,7},{7,4},{8,9},{9,10},{10,1... | collective-permute-start | bytes 1179656 | tf_op jit(solution)/shard_map/ppermute | solution.py:324
  410.6 60.9 %collective-permute-start.7 = (bf16[256,768]{1,0:T(8,128)(2,1)S(1)}, bf16[256,768]{1,0:T(8,128)(2,1)S(1)}, u32[]{:S(2)}, u32[]{:S(2)}) collective-permute-start(bf16[256,768]{1,0:T(8,128)(2,1)S(1)} %get-tuple-element.80), channel_id=1, source_target_pairs={{0,2},{1,3},{2,0},{3,1},{4,6},{5,7},{6,4},{7,5},{8,10},{9,11},{10,... | collective-permute-start | bytes 1179656 | tf_op jit(solution)/shard_map/ppermute | solution.py:324
  412.3 60.1 %collective-permute-start.8 = (bf16[256,768]{1,0:T(8,128)(2,1)S(1)}, bf16[256,768]{1,0:T(8,128)(2,1)S(1)}, u32[]{:S(2)}, u32[]{:S(2)}) collective-permute-start(bf16[256,768]{1,0:T(8,128)(2,1)S(1)} %get-tuple-element.80), channel_id=1, source_target_pairs={{0,3},{1,0},{2,1},{3,2},{4,7},{5,4},{6,5},{7,6},{8,11},{9,8},{10,9... | collective-permute-start | bytes 1179656 | tf_op jit(solution)/shard_map/ppermute | solution.py:324
  475.0 2.3 copy-start.4
  477.3 1.8 copy-start.8
  477.3 3.0 copy-start.1
Sparse Core Ops, SparseCore 0:
  11.7 93.1 all-gather.5
  150.9 37.4 all-gather.7
  221.4 33.8 reduce-scatter.6
  261.1 143.9 reduce-scatter.8
  406.6 18.0 all-gather.9
